TPU v7x, 256 devices: a whole 4x4x8 slice. The times are simulated.
256 devices in a mesh: zonal: 64 (over y_lo, x, z), merid: 4 (over y_hi, core).
Axes of the slice: x: 4, y: 4 (y_hi: 2, y_lo: 2; y = y_hi * 2 + y_lo), z: 8, core: 2. Of those that a mesh axis runs over, the one named last changes fastest.
Arguments:
- field: bfloat16 [64, 4096, 256], P('merid', 'zonal'), may hold values from -6 to 6
- weight_one: bfloat16 [3, 3, 256, 256], replicated, may hold values from -0.125 to 0.125
- bias_one: float32 [256], replicated, may hold values from -3 to 3
- weight_two: bfloat16 [3, 3, 256, 256], replicated, may hold values from -0.125 to 0.125
- bias_two: float32 [256], replicated, may hold values from -3 to 3
- depth_levels: int32 [64, 4096], P('merid', 'zonal'), may hold values from 0 to 64
- fold_partner: int32 [4096], replicated, may hold values from 0 to 4095, as said below
- cotangent: bfloat16 [64, 4096, 256], P('merid', 'zonal'), may hold values from -6 to 6
Outputs:
- output: bfloat16 [64, 4096, 256], P('merid', 'zonal')
- input_grad: bfloat16 [64, 4096, 256], P('merid', 'zonal')
- grad_one: float32 [3, 3, 256, 256], replicated
- grad_two: float32 [3, 3, 256, 256], replicated
Inputs may be any that keep to these rules, and one draw needn't show every extreme that they name: fold_partner[i] = (4095 - i + s) mod 4096 with one pivot offset s, 0 to 4095, for the whole table.
All inputs are finite; a program needn't handle non-finite values.
Results may differ from a plain program's by a relative error of at most 0.003.
Values may be sent and summed in bfloat16 or wider, within the bound.
No kernel may reach another device: no remote copies, remote signals or barrier semaphores. Data moves between devices by JAX's collectives and lax.ppermute only.
A program may use at most 128 MiB of HBM per device.

v0:
```python
import math
import jax
import jax.numpy as jnp
from jax import lax
from jax.sharding import PartitionSpec as P

LEV = 64


def with_halo(cells, sides, width, closed):
    for axis, dim in sides:
        count = lax.axis_size(axis)
        ends = count if closed else count - 1
        head = lax.slice_in_dim(cells, 0, width, axis=dim)
        tail = lax.slice_in_dim(cells, cells.shape[dim] - width, cells.shape[dim], axis=dim)
        cells = jnp.concatenate(
            [
                lax.ppermute(tail, axis, [(i, (i + 1) % count) for i in range(ends)]),
                cells,
                lax.ppermute(head, axis, [((i + 1) % count, i) for i in range(ends)]),
            ],
            axis=dim,
        )
    return cells


def level_mask(depth_levels, channels):
    level_index = lax.broadcasted_iota(jnp.int32, (1, 1, channels), 2) % LEV
    return (level_index < depth_levels[:, :, None]).astype(jnp.float32)


def fold_forward(top_row, fold_partner):
    columns = top_row.shape[0]
    whole_row = lax.all_gather(top_row, "zonal", axis=0, tiled=True)
    partners = lax.dynamic_slice_in_dim(fold_partner, lax.axis_index("zonal") * columns, columns, 0)
    return jnp.take(whole_row, partners, axis=0)


def fold_backward(fold_grad, fold_partner):
    columns = fold_grad.shape[0]
    whole_row = lax.all_gather(fold_grad.astype(jnp.bfloat16), "zonal", axis=0, tiled=True).astype(
        fold_grad.dtype
    )
    partners = lax.dynamic_slice_in_dim(fold_partner, lax.axis_index("zonal") * columns, columns, 0)
    return jnp.take(whole_row, partners, axis=0)


def pad_field(values, fold_partner, is_top):
    with_rows = with_halo(values, (("merid", 0),), 1, False)
    fold_row = fold_forward(values[-1], fold_partner)
    upper_row = jnp.where(is_top, fold_row, with_rows[-1])
    with_rows = jnp.concatenate([with_rows[:-1], upper_row[None]], axis=0)
    return with_halo(with_rows, (("zonal", 1),), 1, True)


def unpad_grad(grad_pad, fold_partner, is_top):
    sides = jnp.concatenate([grad_pad[:, :1], grad_pad[:, -1:]], axis=1)
    returned = with_halo(sides.astype(jnp.bfloat16), (("zonal", 1),), 1, True).astype(sides.dtype)
    inner = grad_pad[:, 1:-1]
    inner = inner.at[:, 0].add(returned[:, 0]).at[:, -1].add(returned[:, 3])
    rims = jnp.concatenate([inner[:1], inner[-1:]], axis=0)
    back_rows = with_halo(rims.astype(jnp.bfloat16), (("merid", 0),), 1, False).astype(rims.dtype)
    folded = fold_backward(inner[-1], fold_partner)
    top_added = back_rows[3] + jnp.where(is_top, folded, jnp.zeros_like(folded))
    middle = inner[1:-1]
    return middle.at[0].add(back_rows[0]).at[-1].add(top_added)


def patches_of(padded, rows, columns):
    pieces = [
        padded[row_step : row_step + rows, col_step : col_step + columns]
        for row_step in range(3)
        for col_step in range(3)
    ]
    return jnp.concatenate(pieces, axis=2).reshape(rows * columns, -1)


def transpose_conv(delta, flat_weight, rows, columns):
    channels = delta.shape[1]
    parts = lax.dot_general(
        delta, flat_weight, (((1,), (1,)), ((), ())), preferred_element_type=jnp.float32
    )
    parts = parts.reshape(rows, columns, 9, channels)
    grad_pad = jnp.zeros((rows + 2, columns + 2, channels), jnp.float32)
    for row_step in range(3):
        for col_step in range(3):
            grad_pad = grad_pad.at[row_step : row_step + rows, col_step : col_step + columns].add(
                parts[:, :, 3 * row_step + col_step]
            )
    return grad_pad


def kernel_grad(patches, delta):
    channels = delta.shape[1]
    summed = lax.dot_general(
        patches, delta, (((0,), (0,)), ((), ())), preferred_element_type=jnp.float32
    )
    return summed.reshape(3, 3, channels, channels)


def shards(
    field, weight_one, bias_one, weight_two, bias_two, depth_levels, fold_partner, cotangent
):
    rows, columns, channels = field.shape
    is_top = lax.axis_index("merid") == lax.axis_size("merid") - 1
    mask = level_mask(depth_levels, channels)
    flat_one = weight_one.reshape(9 * channels, channels)
    flat_two = weight_two.reshape(9 * channels, channels)
    patches_one = patches_of(pad_field(field, fold_partner, is_top), rows, columns)
    pre_one = (
        jnp.dot(patches_one, flat_one, preferred_element_type=jnp.float32).reshape(
            rows, columns, channels
        )
        + bias_one
    )
    hidden = (jax.nn.gelu(pre_one) * mask).astype(jnp.bfloat16)
    patches_two = patches_of(pad_field(hidden, fold_partner, is_top), rows, columns)
    pre_two = jnp.dot(patches_two, flat_two, preferred_element_type=jnp.float32).reshape(
        rows, columns, channels
    )
    output = ((field.astype(jnp.float32) + pre_two + bias_two) * mask).astype(jnp.bfloat16)
    masked_grad = cotangent.astype(jnp.float32) * mask
    delta_two = masked_grad.astype(jnp.bfloat16).reshape(rows * columns, channels)
    grad_two = kernel_grad(patches_two, delta_two)
    hidden_grad = unpad_grad(
        transpose_conv(delta_two, flat_two, rows, columns), fold_partner, is_top
    )
    _, gelu_back = jax.vjp(jax.nn.gelu, pre_one)
    delta_one = (
        gelu_back(hidden_grad * mask)[0].astype(jnp.bfloat16).reshape(rows * columns, channels)
    )
    grad_one = kernel_grad(patches_one, delta_one)
    field_grad = unpad_grad(
        transpose_conv(delta_one, flat_one, rows, columns), fold_partner, is_top
    )
    input_grad = (masked_grad + field_grad).astype(jnp.bfloat16)
    grad_one, grad_two = lax.psum((grad_one, grad_two), ("zonal", "merid"))
    scale = 1.0 / math.sqrt(rows * columns * lax.axis_size("zonal") * lax.axis_size("merid"))
    return (output, input_grad, grad_one * scale, grad_two * scale)


def solution(mesh):
    placed = (
        P("merid", "zonal", None),
        P(),
        P(),
        P(),
        P(),
        P("merid", "zonal"),
        P(),
        P("merid", "zonal", None),
    )
    return jax.shard_map(
        shards,
        mesh=mesh,
        in_specs=placed,
        out_specs=(P("merid", "zonal", None), P("merid", "zonal", None), P(), P()),
        check_vma=False,
    )
```

profile of v0, /device:TPU:97, one launch (start us, length us, event | category | flops | bytes accessed | tf_op | source)
XLA Modules:
  0.0 1509.0 jit_solution(12286972379343277605)
XLA Ops:
  19.0 6.4 scatter-add.89
  26.8 4.3 add_select_fusion.1
  31.1 6.4 scatter-add.90
  41.3 5.1 scatter-add.94
  48.8 5.1 scatter-add.95
  57.8 5.1 scatter-add.99
  65.3 5.1 scatter-add.100
  83.2 6.8 collective-permute-start
  94.1 5.1 collective-permute-start.10
  101.2 157.8 %all-gather.9.cloned.1.call-done = bf16[1,4096,256]{2,1,0:T(8,128)(2,1)} async-done(((bf16[1,64,256]{2,1,0:T(8,128)(2,1)}), bf16[1,4096,256]{2,1,0:T(8,128)(2,1)}) %all-gather.9.cloned.1.call-update) | async-done | bytes 2097168 | tf_op jit(solution)/shard_map/all_gather | solution.py:34
  262.9 3.3 collective-permute-start.3
  276.2 282.4 %all-gather.13.cloned.1.call-done = bf16[1,4096,256]{2,1,0:T(8,128)(2,1)} async-done(((bf16[1,64,256]{2,1,0:T(8,128)(2,1)}), bf16[1,4096,256]{2,1,0:T(8,128)(2,1)}) %all-gather.13.cloned.1.call-update) | async-done | bytes 2097168 | tf_op jit(solution)/shard_map/all_gather | solution.py:41
  558.5 3.9 bitcast_convert_fusion.1
  565.4 5.2 fusion.8
  574.0 3.4 copy-done.3
  579.7 6.4 scatter-add.110
  586.1 3.3 add_select_fusion
  589.4 3.3 scatter-add.111
  619.2 50.8 %collective-permute-start.5 = (bf16[1,64,256]{2,1,0:T(8,128)(2,1)}, bf16[1,64,256]{2,1,0:T(8,128)(2,1)S(1)}, u32[]{:S(2)}, u32[]{:S(2)}) collective-permute-start(bf16[1,64,256]{2,1,0:T(8,128)(2,1)} %get-tuple-element.341), channel_id=1, source_target_pairs={{1,0},{2,1},{3,2},{5,4},{6,5},{7,6},{9,8},{10,9},{11,10},{13,12},{... | collective-permute-start | bytes 98312 | tf_op jit(solution)/shard_map/ppermute | solution.py:20
  670.0 4.3 collective-permute-start.4
  674.3 6.8 copy.30
  681.1 187.6 %all-gather.11.cloned.1.call-done = bf16[1,4096,256]{2,1,0:T(8,128)(2,1)} async-done(((bf16[1,64,256]{2,1,0:T(8,128)(2,1)}), bf16[1,4096,256]{2,1,0:T(8,128)(2,1)}) %all-gather.11.cloned.1.call-update) | async-done | bytes 2097168 | tf_op jit(solution)/shard_map/all_gather | solution.py:34
  876.0 5.1 fusion.55
  884.6 6.8 copy.31
  891.4 5.1 fusion.56
  897.3 52.6 %collective-permute-start.14 = (bf16[1,64,256]{2,1,0:T(8,128)(2,1)S(1)}, bf16[1,64,256]{2,1,0:T(8,128)(2,1)S(1)}, u32[]{:S(2)}, u32[]{:S(2)}) collective-permute-start(bf16[1,64,256]{2,1,0:T(8,128)(2,1)S(1)} %copy-done.14), channel_id=1, source_target_pairs={{0,1},{1,2},{2,3},{4,5},{5,6},{6,7},{8,9},{9,10},{10,11},{12,13},{... | collective-permute-start | bytes 98312 | tf_op jit(solution)/shard_map/ppermute | solution.py:18
  951.9 4.7 collective-permute-done.15
  956.7 211.5 %all-gather.15.cloned.1.call-done = bf16[1,4096,256]{2,1,0:T(8,128)(2,1)} async-done(((bf16[1,64,256]{2,1,0:T(8,128)(2,1)}), bf16[1,4096,256]{2,1,0:T(8,128)(2,1)}) %all-gather.15.cloned.1.call-update) | async-done | bytes 2097168 | tf_op jit(solution)/shard_map/all_gather | solution.py:41
  1168.2 3.9 bitcast_convert_fusion
  1176.3 4.5 fusion.1
  1180.8 316.5 %all-reduce.5.cloned.1.call-done = (f32[3,3,256,256]{3,2,1,0:T(8,128)}, f32[3,3,256,256]{3,2,1,0:T(8,128)}) async-done(((f32[3,3,256,256]{3,2,1,0:T(8,128)}, f32[3,3,256,256]{3,2,1,0:T(8,128)}), (f32[3,3,256,256]{3,2,1,0:T(8,128)}, f32[3,3,256,256]{3,2,1,0:T(8,128)})) %all-reduce.5.cloned.1.call-update) | async-done | bytes 4718608 | tf_op jit(solution)/shard_map/psum | solution.py:137
  1497.3 5.1 broadcast_multiply_fusion
  (180 shorter events, 110.6 us)
Async XLA Ops:
  7.2 558.2 %copy-start = (bf16[3,3,256,256]{3,2,1,0:T(8,128)(2,1)S(1)}, bf16[3,3,256,256]{3,2,1,0:T(8,128)(2,1)}, u32[]{:S(2)}) copy-start(bf16[3,3,256,256]{3,2,1,0:T(8,128)(2,1)} %param.65) | copy-start | bytes 3538948
  7.2 251.8 %all-gather.9.cloned.1.call-start = ((), (), s32[]{:S(2)}) async-start(), calls=%async_computation | async-start | bytes 2129920 | tf_op jit(solution)/shard_map/all_gather | solution.py:34
  8.7 549.8 %all-gather.13.cloned.1.call-start = ((), (), s32[]{:S(2)}) async-start(), calls=%async_computation.2 | async-start | bytes 2129920 | tf_op jit(solution)/shard_map/all_gather | solution.py:41
  8.8 556.6 %copy-start.25 = (s32[256]{0:T(256)}, s32[256]{0:T(256)S(1)}, u32[]{:S(2)}) copy-start(s32[256]{0:T(256)S(1)} %and_select_fusion) | copy-start | bytes 3076
  70.5 4.1 collective-permute-start.8
  73.4 3.8 collective-permute-start.9
  83.2 785.5 %all-gather.11.cloned.1.call-start = ((), (), s32[]{:S(2)}) async-start(), calls=%async_computation.1 | async-start | bytes 2129920 | tf_op jit(solution)/shard_map/all_gather | solution.py:34
  83.2 178.4 %collective-permute-start = (bf16[1,64,256]{2,1,0:T(8,128)(2,1)S(1)}, bf16[1,64,256]{2,1,0:T(8,128)(2,1)S(1)}, u32[]{:S(2)}, u32[]{:S(2)}) collective-permute-start(bf16[1,64,256]{2,1,0:T(8,128)(2,1)S(1)} %copy-done.17), channel_id=1, source_target_pairs={{0,1},{1,2},{2,3},{4,5},{5,6},{6,7},{8,9},{9,10},{10,11},{12,13},{... | collective-permute-start | bytes 98312 | tf_op jit(solution)/shard_map/ppermute | solution.py:18
  90.1 171.5 %collective-permute-start.1 = (bf16[1,64,256]{2,1,0:T(8,128)(2,1)S(1)}, bf16[1,64,256]{2,1,0:T(8,128)(2,1)S(1)}, u32[]{:S(2)}, u32[]{:S(2)}) collective-permute-start(bf16[1,64,256]{2,1,0:T(8,128)(2,1)S(1)} %get-tuple-element.343), channel_id=1, source_target_pairs={{1,0},{2,1},{3,2},{5,4},{6,5},{7,6},{9,8},{10,9},{11,10},{13,12},{... | collective-permute-start | bytes 98312 | tf_op jit(solution)/shard_map/ppermute | solution.py:20
  92.8 472.5 %copy-start.22 = (pred[64]{0:T(512)(128)(4,1)}, pred[64]{0:T(512)(128)(4,1)S(1)}, u32[]{:S(2)}) copy-start(pred[64]{0:T(512)(128)(4,1)S(1)} %get-tuple-element.320) | copy-start | bytes 196
  92.8 469.7 %copy-start.24 = (s32[1024]{0:T(1024)}, s32[1024]{0:T(1024)S(1)}, u32[]{:S(2)}) copy-start(s32[1024]{0:T(1024)S(1)} %pad_clamp_fusion) | copy-start | bytes 12292
  94.1 172.1 %collective-permute-start.10 = (bf16[1,64,256]{2,1,0:T(8,128)(2,1)}, bf16[1,64,256]{2,1,0:T(8,128)(2,1)S(1)}, u32[]{:S(2)}, u32[]{:S(2)}) collective-permute-start(bf16[1,64,256]{2,1,0:T(8,128)(2,1)} %get-tuple-element.324), channel_id=1, source_target_pairs={{0,1},{1,2},{2,3},{4,5},{5,6},{6,7},{8,9},{9,10},{10,11},{12,13},{... | collective-permute-start | bytes 98312 | tf_op jit(solution)/shard_map/ppermute | solution.py:18
  99.3 167.0 %collective-permute-start.11 = (bf16[1,64,256]{2,1,0:T(8,128)(2,1)S(1)}, bf16[1,64,256]{2,1,0:T(8,128)(2,1)S(1)}, u32[]{:S(2)}, u32[]{:S(2)}) collective-permute-start(bf16[1,64,256]{2,1,0:T(8,128)(2,1)S(1)} %get-tuple-element.325), channel_id=1, source_target_pairs={{1,0},{2,1},{3,2},{5,4},{6,5},{7,6},{9,8},{10,9},{11,10},{13,12},{... | collective-permute-start | bytes 98312 | tf_op jit(solution)/shard_map/ppermute | solution.py:20
  261.7 5.7 collective-permute-start.2
  262.9 4.4 collective-permute-start.3
  276.2 289.3 %copy-start.20 = (s32[16,64]{1,0:T(8,128)S(1)}, s32[16,64]{1,0:T(8,128)}, u32[]{:S(2)}) copy-start(s32[16,64]{1,0:T(8,128)} %param.69) | copy-start | bytes 12292
  276.2 289.3 %copy-start.28 = (f32[256]{0:T(256)S(1)}, f32[256]{0:T(256)}, u32[]{:S(2)}) copy-start(f32[256]{0:T(256)} %param.66) | copy-start | bytes 3076
  571.2 596.9 %all-gather.15.cloned.1.call-start = ((), (), s32[]{:S(2)}) async-start(), calls=%async_computation.3 | async-start | bytes 2129920 | tf_op jit(solution)/shard_map/all_gather | solution.py:41
  609.3 5.5 collective-permute-start.12
  610.6 4.2 collective-permute-start.13
  619.1 878.2 %all-reduce.5.cloned.1.call-start = ((), (), s32[]{:S(2)}) async-start(), calls=%async_computation.4 | async-start | bytes 9437184 | tf_op jit(solution)/shard_map/psum | solution.py:137
  619.2 252.2 %collective-permute-start.5 = (bf16[1,64,256]{2,1,0:T(8,128)(2,1)}, bf16[1,64,256]{2,1,0:T(8,128)(2,1)S(1)}, u32[]{:S(2)}, u32[]{:S(2)}) collective-permute-start(bf16[1,64,256]{2,1,0:T(8,128)(2,1)} %get-tuple-element.341), channel_id=1, source_target_pairs={{1,0},{2,1},{3,2},{5,4},{6,5},{7,6},{9,8},{10,9},{11,10},{13,12},{... | collective-permute-start | bytes 98312 | tf_op jit(solution)/shard_map/ppermute | solution.py:20
  670.0 201.4 %collective-permute-start.4 = (bf16[1,64,256]{2,1,0:T(8,128)(2,1)}, bf16[1,64,256]{2,1,0:T(8,128)(2,1)S(1)}, u32[]{:S(2)}, u32[]{:S(2)}) collective-permute-start(bf16[1,64,256]{2,1,0:T(8,128)(2,1)} %get-tuple-element.340), channel_id=1, source_target_pairs={{0,1},{1,2},{2,3},{4,5},{5,6},{6,7},{8,9},{9,10},{10,11},{12,13},{... | collective-permute-start | bytes 98312 | tf_op jit(solution)/shard_map/ppermute | solution.py:18
  674.3 197.0 %copy-start.23 = (pred[64]{0:T(512)(128)(4,1)S(1)}, pred[64]{0:T(512)(128)(4,1)}, u32[]{:S(2)}) copy-start(pred[64]{0:T(512)(128)(4,1)} %copy-done.22) | copy-start | bytes 196
  674.3 201.7 %copy-start.12 = (bf16[16,64,256]{2,1,0:T(8,128)(2,1)S(1)}, bf16[16,64,256]{2,1,0:T(8,128)(2,1)}, u32[]{:S(2)}) copy-start(bf16[16,64,256]{2,1,0:T(8,128)(2,1)} %get-tuple-element.326) | copy-start | bytes 1572868
  871.5 9.7 collective-permute-start.6
  873.5 7.7 collective-permute-start.7
  897.3 54.6 %collective-permute-start.14 = (bf16[1,64,256]{2,1,0:T(8,128)(2,1)S(1)}, bf16[1,64,256]{2,1,0:T(8,128)(2,1)S(1)}, u32[]{:S(2)}, u32[]{:S(2)}) collective-permute-start(bf16[1,64,256]{2,1,0:T(8,128)(2,1)S(1)} %copy-done.14), channel_id=1, source_target_pairs={{0,1},{1,2},{2,3},{4,5},{5,6},{6,7},{8,9},{9,10},{10,11},{12,13},{... | collective-permute-start | bytes 98312 | tf_op jit(solution)/shard_map/ppermute | solution.py:18
  949.9 6.7 collective-permute-start.15
  956.6 218.5 %copy-start.10 = (bf16[16,64,256]{2,1,0:T(8,128)(2,1)S(1)}, bf16[16,64,256]{2,1,0:T(8,128)(2,1)}, u32[]{:S(2)}) copy-start(bf16[16,64,256]{2,1,0:T(8,128)(2,1)} %param.71) | copy-start | bytes 1572868
  956.6 218.5 %copy-start.21 = (s32[16,64]{1,0:T(8,128)S(1)}, s32[16,64]{1,0:T(8,128)}, u32[]{:S(2)}) copy-start(s32[16,64]{1,0:T(8,128)} %param.69) | copy-start | bytes 12292
  956.6 218.5 %copy-start.26 = (s32[256]{0:T(256)S(1)}, s32[256]{0:T(256)}, u32[]{:S(2)}) copy-start(s32[256]{0:T(256)} %copy-done.25) | copy-start | bytes 3076
  (19 other events, 554.1 us)
Sparse Core Ops, SparseCore 0:
  10.4 248.6 all-gather.8
  261.4 297.1 all-gather.12
  571.4 297.2 all-gather.10
  870.3 297.7 all-gather.14
  1174.2 323.0 all-reduce.4
where the time goes:
time: 1510 us
  waiting for transfers between devices  1160 us (77%)
  starting transfers between devices  142 us (9%)
  local copies, waits for them, and re-layouts  106 us (7%)
  other arithmetic  56.4 us (4%)
  matrix products  25.3 us (2%)
    all_gather x2, waiting for transfers between devices, fold_backward(): lax.all_gather(fold_grad.astype(jnp.bfloat16), 'zonal', axis=0, tiled=True)  494 us
    all_gather x2, waiting for transfers between devices, fold_forward(): whole_row = lax.all_gather(top_row, 'zonal', axis=0, tiled=True)  345 us
    psum x1, waiting for transfers between devices, shards(): grad_one, grad_two = lax.psum((grad_one, grad_two), ('zonal', 'merid'))  317 us
    ppermute x8, starting transfers between devices, with_halo(): lax.ppermute(tail, axis, [(i, (i + 1) % count) for i in range(ends)])  76.3 us
    ppermute x8, starting transfers between devices, with_halo(): lax.ppermute(head, axis, [((i + 1) % count, i) for i in range(ends)])  65.5 us
    scatter-add x14, local copies, waits for them, and re-layouts, transpose_conv(): grad_pad.at[row_step:row_step + rows, col_step:col_step + columns]  51.2 us
  transfers between devices with their start and end apart: 21, of which 9 were waited for; matrix products, arithmetic and copies ran while one was open for 10% of the time, Pallas kernels for 0%

commit v1 on v0

--- a/solution.py
+++ b/solution.py
@@ -134,7 +134,9 @@
         transpose_conv(delta_one, flat_one, rows, columns), fold_partner, is_top
     )
     input_grad = (masked_grad + field_grad).astype(jnp.bfloat16)
-    grad_one, grad_two = lax.psum((grad_one, grad_two), ("zonal", "merid"))
+    grad_one, grad_two = lax.psum(
+        lax.psum((grad_one, grad_two), axis_name="merid"), axis_name="zonal"
+    )
     scale = 1.0 / math.sqrt(rows * columns * lax.axis_size("zonal") * lax.axis_size("merid"))
     return (output, input_grad, grad_one * scale, grad_two * scale)
 

time: 1510 us -> 1990 us (1.32)
  the two profiles are of different devices: /device:TPU:97 before, /device:TPU:16 now
where the time goes in v1:
time: 1990 us
  waiting for transfers between devices  1700 us (85%)
  local copies, waits for them, and re-layouts  128 us (6%)
  other arithmetic  65.3 us (3%)
  starting transfers between devices  54.3 us (3%)
  matrix products  23.6 us (1%)
    psum x1, waiting for transfers between devices, shards(): lax.psum(lax.psum((grad_one, grad_two), axis_name='merid'), axis_name='zo...  607 us
    all_gather x2, waiting for transfers between devices, fold_backward(): lax.all_gather(fold_grad.astype(jnp.bfloat16), 'zonal', axis=0, tiled=True)  574 us
    all_gather x2, waiting for transfers between devices, fold_forward(): whole_row = lax.all_gather(top_row, 'zonal', axis=0, tiled=True)  494 us
    scatter-add x14, local copies, waits for them, and re-layouts, transpose_conv(): grad_pad.at[row_step:row_step + rows, col_step:col_step + columns]  67.1 us
    ppermute x8, starting transfers between devices, with_halo(): lax.ppermute(head, axis, [((i + 1) % count, i) for i in range(ends)])  41.5 us
  transfers between devices with their start and end apart: 22, of which 10 were waited for; matrix products, arithmetic and copies ran while one was open for 9% of the time, Pallas kernels for 0%

profile of v1, /device:TPU:16, one launch (start us, length us, event | category | flops | bytes accessed | tf_op | source)
XLA Modules:
  0.0 1990.2 jit_solution(17625220805685448609)
XLA Ops:
  18.9 6.4 scatter-add.89
  31.1 6.5 scatter-add.90
  41.4 5.1 scatter-add.94
  48.9 5.1 scatter-add.95
  57.8 5.1 scatter-add.99
  65.3 5.1 scatter-add.100
  72.6 6.9 collective-permute-start.9
  90.9 5.1 collective-permute-start.1
  100.1 5.1 collective-permute-start.11
  105.3 207.7 %all-gather.9.cloned.1.call-done = bf16[1,4096,256]{2,1,0:T(8,128)(2,1)} async-done(((bf16[1,64,256]{2,1,0:T(8,128)(2,1)}), bf16[1,4096,256]{2,1,0:T(8,128)(2,1)}) %all-gather.9.cloned.1.call-update) | async-done | bytes 2097168 | tf_op jit(solution)/shard_map/all_gather | solution.py:34
  316.2 5.7 collective-permute-start.3
  332.6 279.8 %all-gather.13.cloned.1.call-done = bf16[1,4096,256]{2,1,0:T(8,128)(2,1)} async-done(((bf16[1,64,256]{2,1,0:T(8,128)(2,1)}), bf16[1,4096,256]{2,1,0:T(8,128)(2,1)}) %all-gather.13.cloned.1.call-update) | async-done | bytes 2097168 | tf_op jit(solution)/shard_map/all_gather | solution.py:41
  620.3 4.7 fusion.8
  630.0 6.7 copy.30
  636.6 286.3 %all-gather.11.cloned.1.call-done = bf16[1,4096,256]{2,1,0:T(8,128)(2,1)} async-done(((bf16[1,64,256]{2,1,0:T(8,128)(2,1)}), bf16[1,4096,256]{2,1,0:T(8,128)(2,1)}) %all-gather.11.cloned.1.call-update) | async-done | bytes 2097168 | tf_op jit(solution)/shard_map/all_gather | solution.py:34
  926.3 5.6 collective-permute-start.7
  931.9 5.1 fusion.55
  940.5 6.7 copy.31
  947.2 5.1 fusion.56
  960.2 6.4 scatter-add.110
  971.0 6.5 scatter-add.111
  981.3 5.1 scatter-add.115
  988.8 5.1 scatter-add.116
  997.8 5.1 scatter-add.120
  1005.3 5.1 scatter-add.121
  1010.7 6.2 collective-permute-start.13
  1024.8 26.6 %all-reduce.9.cloned.1.call-done = (f32[3,3,256,256]{3,2,1,0:T(8,128)}, f32[3,3,256,256]{3,2,1,0:T(8,128)}) async-done(((f32[3,3,256,256]{3,2,1,0:T(8,128)}, f32[3,3,256,256]{3,2,1,0:T(8,128)}), (f32[3,3,256,256]{3,2,1,0:T(8,128)}, f32[3,3,256,256]{3,2,1,0:T(8,128)})) %all-reduce.9.cloned.1.call-update) | async-done | bytes 4718608 | tf_op jit(solution)/shard_map/psum | solution.py:138
  1054.8 4.7 collective-permute-start.15
  1061.8 293.9 %all-gather.15.cloned.1.call-done = bf16[1,4096,256]{2,1,0:T(8,128)(2,1)} async-done(((bf16[1,64,256]{2,1,0:T(8,128)(2,1)}), bf16[1,4096,256]{2,1,0:T(8,128)(2,1)}) %all-gather.15.cloned.1.call-update) | async-done | bytes 2097168 | tf_op jit(solution)/shard_map/all_gather | solution.py:41
  1366.5 4.5 fusion.1
  1371.1 607.3 %all-reduce.7.cloned.1.call-done = (f32[3,3,256,256]{3,2,1,0:T(8,128)}, f32[3,3,256,256]{3,2,1,0:T(8,128)}) async-done(((f32[3,3,256,256]{3,2,1,0:T(8,128)}, f32[3,3,256,256]{3,2,1,0:T(8,128)}), (f32[3,3,256,256]{3,2,1,0:T(8,128)}, f32[3,3,256,256]{3,2,1,0:T(8,128)})) %all-reduce.7.cloned.1.call-update) | async-done | bytes 4718608 | tf_op jit(solution)/shard_map/psum | solution.py:137
  1978.4 5.0 broadcast_multiply_fusion
  (179 shorter events, 129.7 us)
Async XLA Ops:
  7.2 613.1 %copy-start = (bf16[3,3,256,256]{3,2,1,0:T(8,128)(2,1)S(1)}, bf16[3,3,256,256]{3,2,1,0:T(8,128)(2,1)}, u32[]{:S(2)}) copy-start(bf16[3,3,256,256]{3,2,1,0:T(8,128)(2,1)} %param.65) | copy-start | bytes 3538948
  7.2 305.8 %all-gather.9.cloned.1.call-start = ((), (), s32[]{:S(2)}) async-start(), calls=%async_computation | async-start | bytes 2129920 | tf_op jit(solution)/shard_map/all_gather | solution.py:34
  8.7 603.7 %all-gather.13.cloned.1.call-start = ((), (), s32[]{:S(2)}) async-start(), calls=%async_computation.2 | async-start | bytes 2129920 | tf_op jit(solution)/shard_map/all_gather | solution.py:41
  70.6 10.6 collective-permute-start.8
  72.6 8.6 collective-permute-start.9
  88.9 834.0 %all-gather.11.cloned.1.call-start = ((), (), s32[]{:S(2)}) async-start(), calls=%async_computation.1 | async-start | bytes 2129920 | tf_op jit(solution)/shard_map/all_gather | solution.py:34
  89.0 226.6 %collective-permute-start = (bf16[1,64,256]{2,1,0:T(8,128)(2,1)}, bf16[1,64,256]{2,1,0:T(8,128)(2,1)S(1)}, u32[]{:S(2)}, u32[]{:S(2)}) collective-permute-start(bf16[1,64,256]{2,1,0:T(8,128)(2,1)} %get-tuple-element.344), channel_id=1, source_target_pairs={{0,1},{1,2},{2,3},{4,5},{5,6},{6,7},{8,9},{9,10},{10,11},{12,13},{... | collective-permute-start | bytes 98312 | tf_op jit(solution)/shard_map/ppermute | solution.py:18
  90.9 224.6 %collective-permute-start.1 = (bf16[1,64,256]{2,1,0:T(8,128)(2,1)}, bf16[1,64,256]{2,1,0:T(8,128)(2,1)S(1)}, u32[]{:S(2)}, u32[]{:S(2)}) collective-permute-start(bf16[1,64,256]{2,1,0:T(8,128)(2,1)} %get-tuple-element.345), channel_id=1, source_target_pairs={{1,0},{2,1},{3,2},{5,4},{6,5},{7,6},{9,8},{10,9},{11,10},{13,12},{... | collective-permute-start | bytes 98312 | tf_op jit(solution)/shard_map/ppermute | solution.py:20
  96.8 828.6 %copy-start.19 = (pred[64]{0:T(512)(128)(4,1)}, pred[64]{0:T(512)(128)(4,1)S(1)}, u32[]{:S(2)}) copy-start(pred[64]{0:T(512)(128)(4,1)S(1)} %get-tuple-element.322) | copy-start | bytes 196
  96.9 826.1 %copy-start.21 = (s32[1024]{0:T(1024)}, s32[1024]{0:T(1024)S(1)}, u32[]{:S(2)}) copy-start(s32[1024]{0:T(1024)S(1)} %pad_clamp_fusion) | copy-start | bytes 12292
  98.2 223.8 %collective-permute-start.10 = (bf16[1,64,256]{2,1,0:T(8,128)(2,1)}, bf16[1,64,256]{2,1,0:T(8,128)(2,1)S(1)}, u32[]{:S(2)}, u32[]{:S(2)}) collective-permute-start(bf16[1,64,256]{2,1,0:T(8,128)(2,1)} %get-tuple-element.326), channel_id=1, source_target_pairs={{0,1},{1,2},{2,3},{4,5},{5,6},{6,7},{8,9},{9,10},{10,11},{12,13},{... | collective-permute-start | bytes 98312 | tf_op jit(solution)/shard_map/ppermute | solution.py:18
  100.1 221.8 %collective-permute-start.11 = (bf16[1,64,256]{2,1,0:T(8,128)(2,1)S(1)}, bf16[1,64,256]{2,1,0:T(8,128)(2,1)S(1)}, u32[]{:S(2)}, u32[]{:S(2)}) collective-permute-start(bf16[1,64,256]{2,1,0:T(8,128)(2,1)S(1)} %get-tuple-element.327), channel_id=1, source_target_pairs={{1,0},{2,1},{3,2},{5,4},{6,5},{7,6},{9,8},{10,9},{11,10},{13,12},{... | collective-permute-start | bytes 98312 | tf_op jit(solution)/shard_map/ppermute | solution.py:20
  315.6 8.1 collective-permute-start.2
  316.2 7.5 collective-permute-start.3
  332.6 287.6 %copy-start.26 = (f32[256]{0:T(256)S(1)}, f32[256]{0:T(256)}, u32[]{:S(2)}) copy-start(f32[256]{0:T(256)} %param.66) | copy-start | bytes 3076
  625.6 425.7 %all-reduce.9.cloned.1.call-start = ((), (), s32[]{:S(2)}) async-start(), calls=%async_computation.5 | async-start | bytes 9437184 | tf_op jit(solution)/shard_map/psum | solution.py:138
  625.6 299.8 %collective-permute-start.5 = (bf16[1,64,256]{2,1,0:T(8,128)(2,1)S(1)}, bf16[1,64,256]{2,1,0:T(8,128)(2,1)S(1)}, u32[]{:S(2)}, u32[]{:S(2)}) collective-permute-start(bf16[1,64,256]{2,1,0:T(8,128)(2,1)S(1)} %get-tuple-element.343), channel_id=1, source_target_pairs={{1,0},{2,1},{3,2},{5,4},{6,5},{7,6},{9,8},{10,9},{11,10},{13,12},{... | collective-permute-start | bytes 98312 | tf_op jit(solution)/shard_map/ppermute | solution.py:20
  627.6 298.0 %collective-permute-start.4 = (bf16[1,64,256]{2,1,0:T(8,128)(2,1)}, bf16[1,64,256]{2,1,0:T(8,128)(2,1)S(1)}, u32[]{:S(2)}, u32[]{:S(2)}) collective-permute-start(bf16[1,64,256]{2,1,0:T(8,128)(2,1)} %get-tuple-element.342), channel_id=1, source_target_pairs={{0,1},{1,2},{2,3},{4,5},{5,6},{6,7},{8,9},{9,10},{10,11},{12,13},{... | collective-permute-start | bytes 98312 | tf_op jit(solution)/shard_map/ppermute | solution.py:18
  925.6 11.5 collective-permute-start.6
  926.3 10.8 collective-permute-start.7
  952.4 403.3 %all-gather.15.cloned.1.call-start = ((), (), s32[]{:S(2)}) async-start(), calls=%async_computation.3 | async-start | bytes 2129920 | tf_op jit(solution)/shard_map/all_gather | solution.py:41
  1010.6 8.2 collective-permute-start.12
  1010.7 8.1 collective-permute-start.13
  1024.7 953.6 %all-reduce.7.cloned.1.call-start = ((), (), s32[]{:S(2)}) async-start(), calls=%async_computation.4 | async-start | bytes 9437184 | tf_op jit(solution)/shard_map/psum | solution.py:137
  1052.1 8.6 collective-permute-start.14
  1054.8 6.3 collective-permute-start.15
  1060.7 295.0 %copy-start.13 = (bf16[1,64,256]{2,1,0:T(8,128)(2,1)}, bf16[1,64,256]{2,1,0:T(8,128)(2,1)S(1)}, u32[]{:S(2)}) copy-start(bf16[1,64,256]{2,1,0:T(8,128)(2,1)S(1)} %collective-permute-done.14) | copy-start | bytes 98308
  1061.1 294.5 %copy-start.14 = (bf16[1,64,256]{2,1,0:T(8,128)(2,1)}, bf16[1,64,256]{2,1,0:T(8,128)(2,1)S(1)}, u32[]{:S(2)}) copy-start(bf16[1,64,256]{2,1,0:T(8,128)(2,1)S(1)} %collective-permute-done.15) | copy-start | bytes 98308
  1061.8 300.9 %copy-start.20 = (pred[64]{0:T(512)(128)(4,1)S(1)}, pred[64]{0:T(512)(128)(4,1)}, u32[]{:S(2)}) copy-start(pred[64]{0:T(512)(128)(4,1)} %copy-done.19) | copy-start | bytes 196
  1061.8 302.5 %copy-start.6 = (bf16[16,64,256]{2,1,0:T(8,128)(2,1)S(1)}, bf16[16,64,256]{2,1,0:T(8,128)(2,1)}, u32[]{:S(2)}) copy-start(bf16[16,64,256]{2,1,0:T(8,128)(2,1)} %param.71) | copy-start | bytes 1572868
  1061.8 302.5 %copy-start.18 = (s32[16,64]{1,0:T(8,128)S(1)}, s32[16,64]{1,0:T(8,128)}, u32[]{:S(2)}) copy-start(s32[16,64]{1,0:T(8,128)} %param.69) | copy-start | bytes 12292
  1061.8 302.5 %copy-start.24 = (s32[256]{0:T(256)S(1)}, s32[256]{0:T(256)}, u32[]{:S(2)}) copy-start(s32[256]{0:T(256)} %copy-done.22) | copy-start | bytes 3076
  (18 other events, 1117.5 us)
Sparse Core Ops, SparseCore 0:
  10.3 302.5 all-gather.8
  315.3 297.0 all-gather.12
  625.7 297.1 all-gather.10
  952.5 98.8 all-reduce.8
  1053.5 302.0 all-gather.14
  1358.2 620.0 all-reduce.6
